TPU v7x, 32 devices: a whole 2x2x4 slice. The times are simulated.
32 devices in a mesh: dp: 8 (over y, x, core), mp: 4 (over z).
Axes of the slice: x: 2, y: 2, z: 4, core: 2. Of those that a mesh axis runs over, the one named last changes fastest.
Arguments:
- tokens: bfloat16 [20480, 1024], P(('dp', 'mp')), may hold values from -6 to 6
- context: int32 [40], P('dp'), may hold values from 0 to 475, as said below
- timestep: int32 [40], P('dp'), may hold values from 1 to 5000
- time_weight: float32 [1024], replicated, may hold values from -6 to 6
- time_bias: float32 [1024], replicated, may hold values from -3 to 3
- qkv_weight: bfloat16 [3, 1024, 1024], P(None, 'dp', 'mp'), may hold values from -0.1875 to 0.1875
- qv_bias: bfloat16 [16, 128], P('mp', 'dp'), may hold values from -3 to 3
- out_weight: bfloat16 [1024, 1024], P('mp', 'dp'), may hold values from -1 to 1
- out_bias: float32 [1024], replicated, may hold values from -3 to 3
- gain_one: float32 [1024], replicated, may hold values from 0.5 to 1.5
- shift_one: float32 [1024], replicated, may hold values from -3 to 3
- up_weight: bfloat16 [4096, 1024], P('mp', 'dp'), may hold values from -0.1875 to 0.1875
- up_bias: bfloat16 [32, 128], P('mp', 'dp'), may hold values from -3 to 3
- down_weight: bfloat16 [4096, 1024], P('mp', 'dp'), may hold values from -0.09375 to 0.09375
- down_bias: float32 [1024], replicated, may hold values from -3 to 3
- gain_two: float32 [1024], replicated, may hold values from 0.5 to 1.5
- shift_two: float32 [1024], replicated, may hold values from -3 to 3
- cotangent: bfloat16 [20480, 1024], P(('dp', 'mp')), may hold values from -6 to 6
Outputs:
- layer_out: bfloat16 [20480, 1024], P(('dp', 'mp'))
- grad_tokens: float32 [20480, 1024], P(('dp', 'mp'))
- grad_time_weight: float32 [1024], P(('dp', 'mp'))
- grad_time_bias: float32 [1024], P(('dp', 'mp'))
- grad_qkv_weight: float32 [3, 1024, 1024], P(None, 'dp', 'mp')
- grad_qv_bias: float32 [16, 128], P('mp', 'dp')
- grad_out_weight: float32 [1024, 1024], P('mp', 'dp')
- grad_out_bias: float32 [1024], P(('dp', 'mp'))
- grad_gain_one: float32 [1024], P(('dp', 'mp'))
- grad_shift_one: float32 [1024], P(('dp', 'mp'))
- grad_up_weight: float32 [4096, 1024], P('mp', 'dp')
- grad_up_bias: float32 [32, 128], P('mp', 'dp')
- grad_down_weight: float32 [4096, 1024], P('mp', 'dp')
- grad_down_bias: float32 [1024], P(('dp', 'mp'))
- grad_gain_two: float32 [1024], P(('dp', 'mp'))
- grad_shift_two: float32 [1024], P(('dp', 'mp'))
Inputs may be any that keep to these rules, and one draw needn't show every extreme that they name: Sequence b holds context[b] context tokens followed by 25 block tokens; its remaining positions are padding and are never attended to.
All inputs are finite; a program needn't handle non-finite values.
Results may differ from a plain program's by a relative error of at most 0.019.
Values may be sent and summed in bfloat16 or wider, within the bound.
A program may use at most 128 MiB of HBM per device.

v0:
```python
import math
import jax
import jax.numpy as jnp
from jax import lax
from jax.sharding import PartitionSpec as P

BLOCK = 25
TSTEPS = 5000
LN_EPS = 1e-05
MASKED = -1e30


def layer_norm(values_in, gain, shift):
    average = jnp.mean(values_in, axis=-1, keepdims=True)
    centred = values_in - average
    variance = jnp.mean(centred * centred, axis=-1, keepdims=True)
    return centred * lax.rsqrt(variance + LN_EPS) * gain + shift


def gelu_exact(values_in):
    return jax.nn.gelu(values_in, approximate=False)


def times_rows(left, right):
    return lax.dot_general(
        left, right, (((1,), (1,)), ((), ())), preferred_element_type=jnp.float32
    )


def times_cols(left, right):
    return lax.dot_general(
        left, right, (((0,), (0,)), ((), ())), preferred_element_type=jnp.float32
    )


def key_scores(queries, key_rows, live_len):
    head_size = queries.shape[-1]
    scores = jnp.einsum("qhd,khd->hqk", queries, key_rows, preferred_element_type=jnp.float32)
    scores = scores * (1.0 / math.sqrt(head_size))
    usable = jnp.arange(key_rows.shape[0]) < live_len
    return jnp.where(usable[None, None, :], scores, MASKED)


def forward_keys(key_count, record):
    seq_block, live_len = record
    queries = seq_block[:, 0]
    key_rows = seq_block[:key_count, 1]
    values = seq_block[:key_count, 2]
    scores = key_scores(queries, key_rows, live_len)
    row_max = jnp.max(scores, axis=-1, keepdims=True)
    expo_vals = jnp.exp(scores - row_max)
    total_e = jnp.sum(expo_vals, axis=-1, keepdims=True)
    prob_low = (expo_vals / total_e).astype(jnp.bfloat16)
    mixed_out = jnp.einsum("hqk,khd->qhd", prob_low, values, preferred_element_type=jnp.float32)
    return (mixed_out.astype(jnp.bfloat16), (row_max + jnp.log(total_e))[..., 0])


def backward_keys(key_count, record):
    seq_block, live_len, log_total, grad_out = record
    queries = seq_block[:, 0]
    key_rows = seq_block[:key_count, 1]
    values = seq_block[:key_count, 2]
    scale_factor = 1.0 / math.sqrt(queries.shape[-1])
    scores = key_scores(queries, key_rows, live_len)
    probs = jnp.exp(scores - log_total[..., None])
    grad_v = jnp.einsum(
        "hqk,qhd->khd", probs.astype(jnp.bfloat16), grad_out, preferred_element_type=jnp.float32
    )
    grad_p = jnp.einsum("qhd,khd->hqk", grad_out, values, preferred_element_type=jnp.float32)
    inner = jnp.sum(probs * grad_p, axis=-1, keepdims=True)
    grad_s = (probs * (grad_p - inner)).astype(jnp.bfloat16)
    grad_q = (
        jnp.einsum("hqk,khd->qhd", grad_s, key_rows, preferred_element_type=jnp.float32)
        * scale_factor
    )
    grad_k = (
        jnp.einsum("hqk,qhd->khd", grad_s, queries, preferred_element_type=jnp.float32)
        * scale_factor
    )
    return jnp.stack(
        [grad_q.astype(jnp.bfloat16), grad_k.astype(jnp.bfloat16), grad_v.astype(jnp.bfloat16)],
        axis=1,
    )


def body(
    tokens,
    context,
    timestep,
    time_weight,
    time_bias,
    qkv_weight,
    qv_bias,
    out_weight,
    out_bias,
    gain_one,
    shift_one,
    up_weight,
    up_bias,
    down_weight,
    down_bias,
    gain_two,
    shift_two,
    cotangent,
):
    mp_count = lax.axis_size("mp")
    mp_index = lax.axis_index("mp")
    shard_rows = tokens.shape[0]
    seq_count = context.shape[0]
    total_rows = shard_rows * mp_count
    seq_len = total_rows // seq_count
    qkv_weight, out_weight, qv_bias, up_weight, down_weight, up_bias = (
        lax.all_gather(qkv_weight, "dp", axis=1, tiled=True),
        lax.all_gather(out_weight, "dp", axis=1, tiled=True),
        lax.all_gather(qv_bias, "dp", axis=1, tiled=True),
        lax.all_gather(up_weight, "dp", axis=1, tiled=True),
        lax.all_gather(down_weight, "dp", axis=1, tiled=True),
        lax.all_gather(up_bias, "dp", axis=1, tiled=True),
    )
    local_width = qkv_weight.shape[2]
    local_heads = qv_bias.shape[0]
    head_size = qv_bias.shape[1] // 2
    row_ids = mp_index * shard_rows + jnp.arange(shard_rows, dtype=jnp.int32)
    owner = (row_ids // seq_len)[:, None] == jnp.arange(seq_count, dtype=jnp.int32)[None, :]
    frac_table = timestep.astype(jnp.float32) / TSTEPS
    fraction = jnp.sum(jnp.where(owner, frac_table[None, :], 0.0), axis=1)
    h_zero = tokens.astype(jnp.float32) + fraction[:, None] * time_weight + time_bias
    h_low = h_zero.astype(jnp.bfloat16)
    h_all = lax.all_gather(h_low, "mp", axis=0, tiled=True)
    bias_f = qv_bias.astype(jnp.float32)
    qkv_bias = jnp.stack(
        [
            bias_f[:, :head_size].reshape(local_width),
            jnp.zeros((local_width,), jnp.float32),
            bias_f[:, head_size:].reshape(local_width),
        ]
    )
    qkv_rows = (
        jnp.einsum("td,cde->tce", h_all, qkv_weight, preferred_element_type=jnp.float32) + qkv_bias
    ).astype(jnp.bfloat16)
    live_all = context + BLOCK
    seq_qkv = qkv_rows.reshape(seq_count, seq_len, 3, local_heads, head_size)
    mixed_seq, log_totals = lax.map(
        lambda record: forward_keys(seq_len, record), (seq_qkv, live_all)
    )
    attn_flat = mixed_seq.reshape(total_rows, local_width)
    branch_a = (
        lax.psum_scatter(
            jnp.dot(attn_flat, out_weight, preferred_element_type=jnp.float32),
            "mp",
            scatter_dimension=0,
            tiled=True,
        )
        + out_bias
    )
    y_one, ln_one_back = jax.vjp(layer_norm, h_zero + branch_a, gain_one, shift_one)
    y_low = y_one.astype(jnp.bfloat16)
    y_all = lax.all_gather(y_low, "mp", axis=0, tiled=True)
    pre_act = times_rows(y_all, up_weight) + up_bias.reshape(-1).astype(jnp.float32)
    hidden, gelu_back = jax.vjp(gelu_exact, pre_act)
    hidden_low = hidden.astype(jnp.bfloat16)
    branch_f = (
        lax.psum_scatter(
            jnp.dot(hidden_low, down_weight, preferred_element_type=jnp.float32).astype(
                jnp.bfloat16
            ),
            "mp",
            scatter_dimension=0,
            tiled=True,
        ).astype(jnp.float32)
        + down_bias
    )
    y_two, ln_two_back = jax.vjp(layer_norm, y_one + branch_f, gain_two, shift_two)
    layer_out = y_two.astype(jnp.bfloat16)
    grad_z2, grad_gain_two, grad_shift_two = ln_two_back(cotangent.astype(jnp.float32))
    grad_f_low = grad_z2.astype(jnp.bfloat16)
    grad_down_bias = jnp.sum(grad_f_low.astype(jnp.float32), axis=0)
    grad_f_all = lax.all_gather(grad_f_low, "mp", axis=0, tiled=True)
    (grad_pre,) = gelu_back(times_rows(grad_f_all, down_weight))
    grad_pre_low = grad_pre.astype(jnp.bfloat16)
    grad_up_weight = times_cols(grad_pre_low, y_all)
    grad_down_weight = times_cols(hidden_low, grad_f_all)
    grad_up_bias = jnp.sum(grad_pre_low.astype(jnp.float32), axis=0).reshape(up_bias.shape)
    grad_y1 = grad_z2 + lax.psum_scatter(
        jnp.dot(grad_pre_low, up_weight, preferred_element_type=jnp.float32).astype(jnp.bfloat16),
        "mp",
        scatter_dimension=0,
        tiled=True,
    ).astype(jnp.float32)
    grad_z1, grad_gain_one, grad_shift_one = ln_one_back(grad_y1)
    grad_a_low = grad_z1.astype(jnp.bfloat16)
    grad_out_bias = jnp.sum(grad_a_low.astype(jnp.float32), axis=0)
    grad_a_all = lax.all_gather(grad_a_low, "mp", axis=0, tiled=True)
    grad_attn = times_rows(grad_a_all, out_weight).astype(jnp.bfloat16)
    grad_out_weight = times_cols(attn_flat, grad_a_all)
    grad_seq = lax.map(
        lambda record: backward_keys(seq_len, record),
        (
            seq_qkv,
            live_all,
            log_totals,
            grad_attn.reshape(seq_count, seq_len, local_heads, head_size),
        ),
    )
    grad_qkv = grad_seq.reshape(total_rows, 3, local_width)
    grad_qkv_weight = jnp.einsum("td,tce->cde", h_all, grad_qkv, preferred_element_type=jnp.float32)
    bias_sums = jnp.sum(grad_qkv.astype(jnp.float32), axis=0)
    grad_qv_bias = jnp.concatenate(
        [
            bias_sums[0].reshape(local_heads, head_size),
            bias_sums[2].reshape(local_heads, head_size),
        ],
        axis=1,
    )
    grad_tokens = grad_z1 + lax.psum_scatter(
        jnp.einsum("tce,cde->td", grad_qkv, qkv_weight, preferred_element_type=jnp.float32).astype(
            jnp.bfloat16
        ),
        "mp",
        scatter_dimension=0,
        tiled=True,
    ).astype(jnp.float32)
    grad_time_weight = jnp.sum(fraction[:, None] * grad_tokens, axis=0)
    grad_time_bias = jnp.sum(grad_tokens, axis=0)
    (
        grad_qkv_weight,
        grad_out_weight,
        grad_qv_bias,
        grad_up_weight,
        grad_down_weight,
        grad_up_bias,
    ) = (
        lax.psum_scatter(grad_qkv_weight, "dp", scatter_dimension=1, tiled=True),
        lax.psum_scatter(grad_out_weight, "dp", scatter_dimension=1, tiled=True),
        lax.psum_scatter(grad_qv_bias, "dp", scatter_dimension=1, tiled=True),
        lax.psum_scatter(grad_up_weight, "dp", scatter_dimension=1, tiled=True),
        lax.psum_scatter(grad_down_weight, "dp", scatter_dimension=1, tiled=True),
        lax.psum_scatter(grad_up_bias, "dp", scatter_dimension=1, tiled=True),
    )
    (
        grad_out_bias,
        grad_gain_one,
        grad_shift_one,
        grad_gain_two,
        grad_shift_two,
        grad_down_bias,
        grad_time_weight,
        grad_time_bias,
    ) = (
        lax.psum_scatter(grad_out_bias, ("dp", "mp"), scatter_dimension=0, tiled=True),
        lax.psum_scatter(grad_gain_one, ("dp", "mp"), scatter_dimension=0, tiled=True),
        lax.psum_scatter(grad_shift_one, ("dp", "mp"), scatter_dimension=0, tiled=True),
        lax.psum_scatter(grad_gain_two, ("dp", "mp"), scatter_dimension=0, tiled=True),
        lax.psum_scatter(grad_shift_two, ("dp", "mp"), scatter_dimension=0, tiled=True),
        lax.psum_scatter(grad_down_bias, ("dp", "mp"), scatter_dimension=0, tiled=True),
        lax.psum_scatter(grad_time_weight, ("dp", "mp"), scatter_dimension=0, tiled=True),
        lax.psum_scatter(grad_time_bias, ("dp", "mp"), scatter_dimension=0, tiled=True),
    )
    return (
        layer_out,
        grad_tokens,
        grad_time_weight,
        grad_time_bias,
        grad_qkv_weight,
        grad_qv_bias,
        grad_out_weight,
        grad_out_bias,
        grad_gain_one,
        grad_shift_one,
        grad_up_weight,
        grad_up_bias,
        grad_down_weight,
        grad_down_bias,
        grad_gain_two,
        grad_shift_two,
    )


def solution(mesh):
    placed = (
        P(("dp", "mp"), None),
        P("dp"),
        P("dp"),
        P(),
        P(),
        P(None, "dp", "mp"),
        P("mp", "dp"),
        P("mp", "dp"),
        P(),
        P(),
        P(),
        P("mp", "dp"),
        P("mp", "dp"),
        P("mp", "dp"),
        P(),
        P(),
        P(),
        P(("dp", "mp"), None),
    )
    return jax.shard_map(
        body,
        mesh=mesh,
        in_specs=placed,
        out_specs=(
            P(("dp", "mp"), None),
            P(("dp", "mp"), None),
            P(("dp", "mp")),
            P(("dp", "mp")),
            P(None, "dp", "mp"),
            P("mp", "dp"),
            P("mp", "dp"),
            P(("dp", "mp")),
            P(("dp", "mp")),
            P(("dp", "mp")),
            P("mp", "dp"),
            P("mp", "dp"),
            P("mp", "dp"),
            P(("dp", "mp")),
            P(("dp", "mp")),
            P(("dp", "mp")),
        ),
        check_vma=False,
    )
```

profile of v0, /device:TPU:0, one launch (start us, length us, event | category | flops | bytes accessed | tf_op | source)
XLA Modules:
  0.0 1414.3 jit_solution(10360146816921266265)
XLA Ops:
  8.8 2.8 fusion.47
  11.7 10.6 all-gather
  22.7 9.8 all_gather.33
  32.5 5.7 all-gather.12.cloned.1.call-done
  38.2 100.2 %all-gather.10.cloned.1.call-done = bf16[2560,1024]{1,0:T(8,128)(2,1)} async-done(((bf16[640,1024]{1,0:T(8,128)(2,1)}), bf16[2560,1024]{1,0:T(8,128)(2,1)}) %all-gather.10.cloned.1.call-update) | async-done | bytes 5242896 | tf_op jit(solution)/shard_map/all_gather | solution.py:129
  138.4 9.2 add_convert_fusion.1
  147.6 12.2 reshape.203
  159.9 12.0 copy.94
  171.9 31.1 %while.22 = (s32[]{:T(128)}, bf16[5,512,4,64]{1,3,2,0:T(8,128)(2,1)S(1)}, f32[5,4,512]{2,1,0:T(4,128)}, bf16[5,512,3,4,64]{1,4,3,2,0:T(8,128)(2,1)}, s32[5]{0:T(128)S(1)}, /*index=5*/s32[]{:T(128)}) while((s32[]{:T(128)}, bf16[5,512,4,64]{1,3,2,0:T(8,128)(2,1)S(1)}, f32[5,4,512]{2,1,0:T(4,128)}, bf16[5,512,3,4,64]{1,4,3,2,0:T(8,128)(2,1)}, ...), condition=%wide.region_4.5_spmd, body=%wide.region_1.4_spmd.sunk | while | flops 281147904 | bytes 15272541 | solution.py:143
  205.5 5.6 fusion.65
  212.2 175.4 %reduce-scatter.15.cloned.1.call-done = f32[640,1024]{1,0:T(8,128)} async-done(((f32[2560,1024]{1,0:T(8,128)}), f32[640,1024]{1,0:T(8,128)}) %reduce-scatter.15.cloned.1.call-update) | async-done | bytes 2621456 | tf_op jit(solution)/shard_map/reduce_scatter | solution.py:148
  387.7 2.9 fusion.63
  391.0 1.5 fusion.48
  393.2 8.9 all-gather.1
  402.2 16.4 %all-gather.16.cloned.1.call-done = bf16[1024,1024]{1,0:T(8,128)(2,1)} async-done(((bf16[1024,128]{1,0:T(8,128)(2,1)}), bf16[1024,1024]{1,0:T(8,128)(2,1)}) %all-gather.16.cloned.1.call-update) | async-done | bytes 2097168 | tf_op jit(solution)/shard_map/all_gather | solution.py:116
  418.6 100.1 %all-gather.14.cloned.1.call-done = bf16[2560,1024]{1,0:T(8,128)(2,1)} async-done(((bf16[640,1024]{1,0:T(8,128)(2,1)}), bf16[2560,1024]{1,0:T(8,128)(2,1)}) %all-gather.14.cloned.1.call-update) | async-done | bytes 5242896 | tf_op jit(solution)/shard_map/all_gather | solution.py:158
  518.6 32.1 %multiply_convert_fusion.1 = (bf16[2560,1024]{1,0:T(8,128)(2,1)}, f32[2560,1024]{1,0:T(8,128)}, f32[2560,1024]{1,0:T(8,128)}) fusion(f32[1024]{0:T(1024)S(1)} %bitcast.187, bf16[2560,1024]{1,0:T(8,128)(2,1)} %all-gather.14.cloned.1.call-done, bf16[1024,1024]{1,0:T(8,128)(2,1)} %all-gather.16.cloned.1.call-done), kind=kOutput, calls=%fused_computation.55 | convolution fusion | flops 5541724160 | bytes 33558528 | tf_op jit(solution)/shard_map/dot_general | solution.py:25
  550.8 10.2 convolution_convert_fusion.1
  561.3 92.0 %reduce-scatter.17.cloned.1.call-done = bf16[640,1024]{1,0:T(8,128)(2,1)} async-done(((bf16[2560,1024]{1,0:T(8,128)(2,1)}), bf16[640,1024]{1,0:T(8,128)(2,1)}) %reduce-scatter.17.cloned.1.call-update) | async-done | bytes 1310736 | tf_op jit(solution)/shard_map/reduce_scatter | solution.py:163
  653.3 2.3 fusion.61
  656.1 1.5 fusion.46
  657.6 2.1 fusion.60
  659.8 1.5 copy-done
  661.3 1.9 convert_reduce_fusion.3
  663.3 98.6 %all-gather.20.cloned.1.call-done = bf16[2560,1024]{1,0:T(8,128)(2,1)} async-done(((bf16[640,1024]{1,0:T(8,128)(2,1)}), bf16[2560,1024]{1,0:T(8,128)(2,1)}) %all-gather.20.cloned.1.call-update) | async-done | bytes 5242896 | tf_op jit(solution)/shard_map/all_gather | solution.py:178
  761.9 16.5 %convert_reduce_fusion = (f32[1024]{0:T(1024)S(1)}, bf16[2560,1024]{1,0:T(8,128)(2,1)S(1)}) fusion(f32[2560,1024]{1,0:T(8,128)} %get-tuple-element.266, f32[2560,1024]{1,0:T(8,128)} %get-tuple-element.278, f32[1024]{0:T(1024)S(1)} %bitcast.188, bf16[2560,1024]{1,0:T(8,128)(2,1)} %all-gather.20.cloned.1.call-done, ...), kind=kOutput, calls=%fused_computation.53 | convolution fusion | flops 5413272576 | bytes 33562624 | tf_op jit(solution)/shard_map/dot_general | solution.py:25
  778.5 2.4 copy-done.27
  780.9 7.3 convolution_convert_fusion
  788.2 92.2 %reduce-scatter.19.cloned.1.call-done = bf16[640,1024]{1,0:T(8,128)(2,1)} async-done(((bf16[2560,1024]{1,0:T(8,128)(2,1)}), bf16[640,1024]{1,0:T(8,128)(2,1)}) %reduce-scatter.19.cloned.1.call-update) | async-done | bytes 1310736 | tf_op jit(solution)/shard_map/reduce_scatter | solution.py:184
  880.5 3.5 multiply_reduce_fusion.1
  885.2 1.5 copy-done.2
  888.9 97.8 %all-gather.22.cloned.1.call-done = bf16[2560,1024]{1,0:T(8,128)(2,1)} async-done(((bf16[640,1024]{1,0:T(8,128)(2,1)}), bf16[2560,1024]{1,0:T(8,128)(2,1)}) %all-gather.22.cloned.1.call-update) | async-done | bytes 5242896 | tf_op jit(solution)/shard_map/all_gather | solution.py:193
  986.7 5.1 convolution_convert_fusion.2
  991.8 4.2 reshape.198
  996.1 3.0 copy.99
  999.1 60.0 %while.23 = (s32[]{:T(128)}, bf16[5,512,3,4,64]{1,4,3,2,0:T(8,128)(2,1)}, bf16[5,512,3,4,64]{1,4,3,2,0:T(8,128)(2,1)}, s32[5]{0:T(128)S(1)}, f32[5,4,512]{2,1,0:...) while((s32[]{:T(128)}, bf16[5,512,3,4,64]{1,4,3,2,0:T(8,128)(2,1)}, ...), condition=%wide.region_18.19_spmd, body=%wide.region_16.18_spmd.sunk | while | flops 689830400 | bytes 37285476 | solution.py:196
  1003.0 2.4 multiply_reduce_fusion.7
  1008.0 2.1 fusion.113
  1015.0 2.4 multiply_reduce_fusion.7
  1020.0 2.1 fusion.113
  1027.0 2.4 multiply_reduce_fusion.7
  1029.4 1.4 multiply_convert_fusion.3
  1032.0 2.1 fusion.113
  1039.0 2.4 multiply_reduce_fusion.7
  1041.4 1.4 multiply_convert_fusion.3
  1044.0 2.1 fusion.113
  1051.0 2.4 multiply_reduce_fusion.7
  1056.0 2.1 fusion.113
  1059.1 2.7 convert_reduce_fusion.1
  1061.9 7.7 copy.100
  1070.3 9.7 reshape.187
  1080.3 9.7 fusion.49
  1090.0 8.3 bitcast_convert_fusion
  1098.4 10.5 fusion.68
  1108.9 10.5 fusion.67
  1119.5 5.9 fusion.66
  1128.2 33.3 %reduce-scatter.23.cloned.1.call-done = f32[3,128,256]{1,2,0:T(8,128)} async-done(((f32[3,1024,256]{1,2,0:T(8,128)}), f32[3,128,256]{1,2,0:T(8,128)}) %reduce-scatter.23.cloned.1.call-update) | async-done | bytes 393232 | tf_op jit(solution)/shard_map/reduce_scatter | solution.py:233
  1161.5 1.9 copy.102
  1163.4 94.1 %reduce-scatter.21.cloned.1.call-done = bf16[640,1024]{1,0:T(8,128)(2,1)} async-done(((bf16[2560,1024]{1,0:T(8,128)(2,1)}), bf16[640,1024]{1,0:T(8,128)(2,1)}) %reduce-scatter.21.cloned.1.call-update) | async-done | bytes 1310736 | tf_op jit(solution)/shard_map/reduce_scatter | solution.py:215
  1257.5 3.4 fusion.58
  1260.9 41.5 %all-reduce.8 = (f32[1024]{0:T(1024)S(1)}, f32[1024]{0:T(1024)S(1)}, f32[1024]{0:T(1024)S(1)}, f32[1024]{0:T(1024)S(1)}, f32[1024]{0:T(1024)S(1)}, /*index=5*/f3...) all-reduce(f32[1024]{0:T(1024)S(1)} %get-tuple-element.220, ...), channel_id=6, replica_groups=mesh['dp'=8,'mp'=4] {'dp','mp'}, use_global_device_ids=true, to_apply=%region_21.22.clone | all-reduce | flops 8192 | bytes 65536
  1307.1 6.0 reduce-scatter.29.cloned.1.call-done
  1313.1 54.8 %reduce-scatter.27.cloned.1.call-done = f32[1024,128]{1,0:T(8,128)} async-done(((f32[1024,1024]{1,0:T(8,128)}), f32[1024,128]{1,0:T(8,128)}) %reduce-scatter.27.cloned.1.call-update) | async-done | bytes 524304 | tf_op jit(solution)/shard_map/reduce_scatter | solution.py:236
  1367.9 39.6 %reduce-scatter.25.cloned.1.call-done = f32[256,128]{1,0:T(8,128)} async-done(((f32[256,1024]{1,0:T(8,128)}), f32[256,128]{1,0:T(8,128)}) %reduce-scatter.25.cloned.1.call-update) | async-done | bytes 131088 | tf_op jit(solution)/shard_map/reduce_scatter | solution.py:234
  (212 shorter events, 85.1 us)
Async XLA Ops:
  7.2 15.5 %copy-start.7 = (bf16[256,128]{1,0:T(8,128)(2,1)S(1)}, bf16[256,128]{1,0:T(8,128)(2,1)}, u32[]{:S(2)}) copy-start(bf16[256,128]{1,0:T(8,128)(2,1)} %param.29) | copy-start | bytes 196612
  7.2 25.3 %copy-start.24 = (s32[5]{0:T(128)S(1)}, s32[5]{0:T(128)}, u32[]{:S(2)}) copy-start(s32[5]{0:T(128)} %param.23) | copy-start | bytes 64
  7.2 31.0 %all-gather.12.cloned.1.call-start = ((), (), s32[]{:S(2)}) async-start(), calls=%async_computation.11 | async-start | bytes 1769472 | tf_op jit(solution)/shard_map/all_gather | solution.py:113
  7.9 130.5 %all-gather.10.cloned.1.call-start = ((), (), s32[]{:S(2)}) async-start(), calls=%async_computation.10 | async-start | bytes 6553600 | tf_op jit(solution)/shard_map/all_gather | solution.py:129
  8.7 378.9 %copy-start.8 = (f32[640]{0:T(1024)}, f32[640]{0:T(1024)S(1)}, u32[]{:S(2)}) copy-start(f32[640]{0:T(1024)S(1)} %select_reduce_fusion) | copy-start | bytes 7684
  11.6 376.0 %reduce-scatter.15.cloned.1.call-start = ((), (), s32[]{:S(2)}) async-start(), calls=%async_computation.12 | async-start | bytes 13107200 | tf_op jit(solution)/shard_map/reduce_scatter | solution.py:148
  203.0 8.0 copy-start.25
  204.5 1.1 copy-start.4
  211.1 176.6 %copy-start.11 = (f32[1024]{0:T(1024)S(1)}, f32[1024]{0:T(1024)}, u32[]{:S(2)}) copy-start(f32[1024]{0:T(1024)} %param.26) | copy-start | bytes 12292
  211.1 176.6 %copy-start.12 = (f32[1024]{0:T(1024)S(1)}, f32[1024]{0:T(1024)}, u32[]{:S(2)}) copy-start(f32[1024]{0:T(1024)} %param.25) | copy-start | bytes 12292
  211.1 176.6 %copy-start.20 = (f32[1024]{0:T(1024)S(1)}, f32[1024]{0:T(1024)}, u32[]{:S(2)}) copy-start(f32[1024]{0:T(1024)} %param.30) | copy-start | bytes 12292
  211.1 207.5 %all-gather.16.cloned.1.call-start = ((), (), s32[]{:S(2)}) async-start(), calls=%async_computation.14 | async-start | bytes 2359296 | tf_op jit(solution)/shard_map/all_gather | solution.py:116
  211.7 179.3 %copy-start.10 = (f32[1024]{0:T(1024)S(1)}, f32[1024]{0:T(1024)}, u32[]{:S(2)}) copy-start(f32[1024]{0:T(1024)} %param.31) | copy-start | bytes 12292
  211.7 179.3 %copy-start.13 = (f32[1024]{0:T(1024)S(1)}, f32[1024]{0:T(1024)}, u32[]{:S(2)}) copy-start(f32[1024]{0:T(1024)} %param.32) | copy-start | bytes 12292
  211.7 306.9 %all-gather.14.cloned.1.call-start = ((), (), s32[]{:S(2)}) async-start(), calls=%async_computation.13 | async-start | bytes 6553600 | tf_op jit(solution)/shard_map/all_gather | solution.py:158
  390.6 2.6 copy-start.21
  392.6 158.2 %all-gather.18.cloned.1.call-start = ((), (), s32[]{:S(2)}) async-start(), calls=%async_computation.15 | async-start | bytes 2359296 | tf_op jit(solution)/shard_map/all_gather | solution.py:117
  393.2 260.2 %reduce-scatter.17.cloned.1.call-start = ((), (), s32[]{:S(2)}) async-start(), calls=%async_computation.16 | async-start | bytes 6553600 | tf_op jit(solution)/shard_map/reduce_scatter | solution.py:163
  561.0 92.3 %copy-start.18 = (f32[1024]{0:T(1024)S(1)}, f32[1024]{0:T(1024)}, u32[]{:S(2)}) copy-start(f32[1024]{0:T(1024)} %param.36) | copy-start | bytes 12292
  561.0 95.1 %copy-start.14 = (f32[1024]{0:T(1024)S(1)}, f32[1024]{0:T(1024)}, u32[]{:S(2)}) copy-start(f32[1024]{0:T(1024)} %param.37) | copy-start | bytes 12292
  561.1 200.9 %all-gather.20.cloned.1.call-start = ((), (), s32[]{:S(2)}) async-start(), calls=%async_computation.17 | async-start | bytes 6553600 | tf_op jit(solution)/shard_map/all_gather | solution.py:178
  653.3 2.8 copy-start.5
  655.7 1.9 copy-start.19
  659.8 1.5 copy-start
  663.2 217.2 %reduce-scatter.19.cloned.1.call-start = ((), (), s32[]{:S(2)}) async-start(), calls=%async_computation.18 | async-start | bytes 6553600 | tf_op jit(solution)/shard_map/reduce_scatter | solution.py:184
  761.9 19.0 %copy-start.22 = (bf16[1024,1024]{1,0:T(8,128)(2,1)S(1)}, bf16[1024,1024]{1,0:T(8,128)(2,1)}, u32[]{:S(2)}) copy-start(bf16[1024,1024]{1,0:T(8,128)(2,1)} %all-gather.16.cloned.1.call-done) | copy-start | bytes 6291460
  778.5 2.4 copy-start.27
  788.2 198.5 %all-gather.22.cloned.1.call-start = ((), (), s32[]{:S(2)}) async-start(), calls=%async_computation.19 | async-start | bytes 6553600 | tf_op jit(solution)/shard_map/all_gather | solution.py:193
  880.5 3.5 copy-start.1
  880.5 3.5 copy-start.6
  885.1 1.5 copy-start.2
  888.0 237.5 %reduce-scatter.33.cloned.1.call-start = ((), (), s32[]{:S(2)}) async-start(), calls=%async_computation.26 | async-start | bytes 73728
  888.8 238.0 %reduce-scatter.31.cloned.1.call-start = ((), (), s32[]{:S(2)}) async-start(), calls=%async_computation.25 | async-start | bytes 73728
  991.8 7.3 copy-start.26
  1080.1 10.0 copy-start.23
  1080.1 81.5 %reduce-scatter.23.cloned.1.call-start = ((), (), s32[]{:S(2)}) async-start(), calls=%async_computation.21 | async-start | bytes 3538944 | tf_op jit(solution)/shard_map/reduce_scatter | solution.py:233
  1090.0 167.5 %reduce-scatter.21.cloned.1.call-start = ((), (), s32[]{:S(2)}) async-start(), calls=%async_computation.20 | async-start | bytes 6553600 | tf_op jit(solution)/shard_map/reduce_scatter | solution.py:215
  1098.3 214.8 %reduce-scatter.29.cloned.1.call-start = ((), (), s32[]{:S(2)}) async-start(), calls=%async_computation.24 | async-start | bytes 4718592 | tf_op jit(solution)/shard_map/reduce_scatter | solution.py:237
  1108.9 259.1 %reduce-scatter.27.cloned.1.call-start = ((), (), s32[]{:S(2)}) async-start(), calls=%async_computation.23 | async-start | bytes 4718592 | tf_op jit(solution)/shard_map/reduce_scatter | solution.py:236
  1119.4 138.1 %copy-start.3 = (f32[640,1024]{1,0:T(8,128)S(1)}, f32[640,1024]{1,0:T(8,128)}, u32[]{:S(2)}) copy-start(f32[640,1024]{1,0:T(8,128)} %copy-done.2) | copy-start | bytes 7864324
  1119.5 138.1 %copy-start.9 = (f32[640]{0:T(1024)S(1)}, f32[640]{0:T(1024)}, u32[]{:S(2)}) copy-start(f32[640]{0:T(1024)} %copy-done.8) | copy-start | bytes 7684
  1119.5 288.1 %reduce-scatter.25.cloned.1.call-start = ((), (), s32[]{:S(2)}) async-start(), calls=%async_computation.22 | async-start | bytes 1179648 | tf_op jit(solution)/shard_map/reduce_scatter | solution.py:234
  1125.4 135.5 %copy-start.15 = (f32[1024]{0:T(1024)S(1)}, f32[1024]{0:T(1024)}, u32[]{:S(2)}) copy-start(f32[1024]{0:T(1024)} %get-tuple-element.216) | copy-start | bytes 12292
  1125.4 135.5 %copy-start.16 = (f32[1024]{0:T(1024)S(1)}, f32[1024]{0:T(1024)}, u32[]{:S(2)}) copy-start(f32[1024]{0:T(1024)} %get-tuple-element.221) | copy-start | bytes 12292
  1125.4 135.5 %copy-start.17 = (f32[1024]{0:T(1024)S(1)}, f32[1024]{0:T(1024)}, u32[]{:S(2)}) copy-start(f32[1024]{0:T(1024)} %get-tuple-element.254) | copy-start | bytes 12292
Sparse Core Ops, SparseCore 0:
  9.9 28.2 all-gather.11
  40.4 98.0 all-gather.9
  211.2 176.3 reduce-scatter.14
  389.4 29.1 all-gather.15
  420.6 98.0 all-gather.13
  520.4 26.4 all-gather.17
  561.2 92.1 reduce-scatter.16
  663.3 98.5 all-gather.19
  788.3 92.0 reduce-scatter.18
  888.1 98.5 all-gather.21
  989.7 31.9 reduce-scatter.32
  1080.2 31.8 reduce-scatter.30
  1115.4 46.0 reduce-scatter.22
  1163.7 93.7 reduce-scatter.20
  1261.3 51.7 reduce-scatter.28
  1316.9 51.0 reduce-scatter.26
  1371.5 35.9 reduce-scatter.24
where the time goes:
time: 1430 us; the launch traced here: 1410 us
  waiting for transfers between devices  1010 us (71%)
  matrix products  175 us (12%)
  local copies, waits for them, and re-layouts  89.3 us (6%)
  blocking collectives  70.7 us (5%)
  other arithmetic  55 us (4%)
  between operations  14.5 us (1%)
    reduce_scatter x1, waiting for transfers between devices, body(): lax.psum_scatter(jnp.dot(attn_flat, out_weight, preferred_element_type=jn...  175 us
    all_gather x1, waiting for transfers between devices, body(): h_all = lax.all_gather(h_low, 'mp', axis=0, tiled=True)  100 us
    all_gather x1, waiting for transfers between devices, body(): y_all = lax.all_gather(y_low, 'mp', axis=0, tiled=True)  100 us
    all_gather x1, waiting for transfers between devices, body(): grad_f_all = lax.all_gather(grad_f_low, 'mp', axis=0, tiled=True)  98.6 us
    all_gather x1, waiting for transfers between devices, body(): grad_a_all = lax.all_gather(grad_a_low, 'mp', axis=0, tiled=True)  97.8 us
    reduce_scatter x1, waiting for transfers between devices, body(): lax.psum_scatter(jnp.einsum('tce,cde->td', grad_qkv, qkv_weight, preferre...  94.1 us
    reduce_scatter x1, waiting for transfers between devices, body(): lax.psum_scatter(jnp.dot(grad_pre_low, up_weight, preferred_element_type=...  92.2 us
    reduce_scatter x1, waiting for transfers between devices, body(): lax.psum_scatter(jnp.dot(hidden_low, down_weight, preferred_element_type=...  92 us
  transfers between devices with their start and end apart: 17, of which 14 were waited for; matrix products, arithmetic and copies ran while one was open for 14% of the time, Pallas kernels for 0%

commit v1 on v0

--- a/solution.py
+++ b/solution.py
@@ -8,6 +8,12 @@
 TSTEPS = 5000
 LN_EPS = 1e-05
 MASKED = -1e30
+
+
+def laid_out(blocks, dim):
+    dims = list(blocks.shape[1:])
+    dims[dim] *= blocks.shape[0]
+    return jnp.moveaxis(blocks, 0, dim).reshape(dims)
 
 
 def layer_norm(values_in, gain, shift):
@@ -126,7 +132,19 @@
     fraction = jnp.sum(jnp.where(owner, frac_table[None, :], 0.0), axis=1)
     h_zero = tokens.astype(jnp.float32) + fraction[:, None] * time_weight + time_bias
     h_low = h_zero.astype(jnp.bfloat16)
-    h_all = lax.all_gather(h_low, "mp", axis=0, tiled=True)
+    peers = lax.axis_size("mp")
+    pairs = [(i, (i + 1) % peers) for i in range(peers)]
+    back = [(b, a) for a, b in pairs]
+    lower, upper = ([], [])
+    for step in range(peers - 1):
+        if step % 2 == 0:
+            lower.append(lax.ppermute(lower[-1] if lower else h_low, "mp", pairs))
+        else:
+            upper.append(lax.ppermute(upper[-1] if upper else h_low, "mp", back))
+    tiles = jnp.stack([*lower[::-1], h_low, *upper])
+    shift_2 = lax.axis_index("mp") - len(lower)
+    tiles = tiles[(jnp.arange(peers) - shift_2) % peers]
+    h_all = laid_out(tiles, 0)
     bias_f = qv_bias.astype(jnp.float32)
     qkv_bias = jnp.stack(
         [

time: 1430 us -> 1400 us (0.979)
  waiting for transfers between devices: 1010 us -> 966 us
    all_gather x1 -> x0, waiting for transfers between devices: 100 us -> none  [body(): h_all = lax.all_gather(h_low, 'mp', axis=0, tiled=True)]
    ppermute x0 -> x3, waiting for transfers between devices: none -> 63.1 us  [the longest x2 48.7 us: body(): lower.append(lax.ppermute(lower[-1] if lower else h_low, 'mp', pairs))]
  transfers between devices with their start and end apart: 17 -> 19, of which waited for: 14 -> 15; matrix products, arithmetic and copies ran while one was open for 14% -> 14% of each run, Pallas kernels for 0% -> 0%
where the time goes in v1:
time: 1400 us; the launch traced here: 1390 us
  waiting for transfers between devices  966 us (69%)
  matrix products  175 us (12%)
  local copies, waits for them, and re-layouts  95.2 us (7%)
  blocking collectives  70.2 us (5%)
  other arithmetic  61.5 us (4%)
  between operations  14.5 us (1%)
    reduce_scatter x1, waiting for transfers between devices, body(): lax.psum_scatter(jnp.dot(attn_flat, out_weight, preferred_element_type=jn...  177 us
    all_gather x1, waiting for transfers between devices, body(): y_all = lax.all_gather(y_low, 'mp', axis=0, tiled=True)  100 us
    all_gather x1, waiting for transfers between devices, body(): grad_f_all = lax.all_gather(grad_f_low, 'mp', axis=0, tiled=True)  98.7 us
    all_gather x1, waiting for transfers between devices, body(): grad_a_all = lax.all_gather(grad_a_low, 'mp', axis=0, tiled=True)  97.8 us
    reduce_scatter x1, waiting for transfers between devices, body(): lax.psum_scatter(jnp.einsum('tce,cde->td', grad_qkv, qkv_weight, preferre...  94.2 us
    reduce_scatter x1, waiting for transfers between devices, body(): lax.psum_scatter(jnp.dot(grad_pre_low, up_weight, preferred_element_type=...  92.2 us
    reduce_scatter x1, waiting for transfers between devices, body(): lax.psum_scatter(jnp.dot(hidden_low, down_weight, preferred_element_type=...  92 us
    reduce_scatter x1, waiting for transfers between devices, body(): lax.psum_scatter(grad_up_weight, 'dp', scatter_dimension=1, tiled=True)  54.8 us
  transfers between devices with their start and end apart: 19, of which 15 were waited for; matrix products, arithmetic and copies ran while one was open for 14% of the time, Pallas kernels for 0%

profile of v1, /device:TPU:0, one launch (start us, length us, event | category | flops | bytes accessed | tf_op | source)
XLA Modules:
  0.0 1388.8 jit_solution(13122092676789800500)
XLA Ops:
  8.1 2.8 fusion.44
  10.9 3.1 collective-permute-start
  14.1 2.1 collective-permute-start.2
  16.2 9.3 all-gather
  25.4 20.5 %collective-permute-done = bf16[640,1024]{1,0:T(8,128)(2,1)S(1)} collective-permute-done((bf16[640,1024]{1,0:T(8,128)(2,1)}, bf16[640,1024]{1,0:T(8,128)(2,1)S(1)}, u32[]{:S(2)}, u32[]{:S(2)}) %collective-permute-start) | collective-permute-done | bytes 1310752 | tf_op jit(solution)/shard_map/ppermute | solution.py:141
  46.3 10.5 all_gather.29
  58.7 14.4 %collective-permute-done.2 = bf16[640,1024]{1,0:T(8,128)(2,1)} collective-permute-done((bf16[640,1024]{1,0:T(8,128)(2,1)}, bf16[640,1024]{1,0:T(8,128)(2,1)}, u32[]{:S(2)}, u32[]{:S(2)}) %collective-permute-start.2) | collective-permute-done | bytes 1310752 | tf_op jit(solution)/shard_map/ppermute | solution.py:143
  73.1 28.2 %collective-permute-done.1 = bf16[640,1024]{1,0:T(8,128)(2,1)} collective-permute-done((bf16[640,1024]{1,0:T(8,128)(2,1)S(1)}, bf16[640,1024]{1,0:T(8,128)(2,1)}, u32[]{:S(2)}, u32[]{:S(2)}) %collective-permute-start.1) | collective-permute-done | bytes 1310752 | tf_op jit(solution)/shard_map/ppermute | solution.py:141
  101.3 4.6 pad_maximum_fusion
  106.0 5.7 gather_fusion
  111.7 9.2 add_convert_fusion.1
  120.9 12.2 reshape.264
  133.1 12.1 copy.94
  145.2 31.1 %while.22 = (s32[]{:T(128)}, bf16[5,512,4,64]{1,3,2,0:T(8,128)(2,1)S(1)}, f32[5,4,512]{2,1,0:T(4,128)}, bf16[5,512,3,4,64]{1,4,3,2,0:T(8,128)(2,1)}, s32[5]{0:T(128)S(1)}, /*index=5*/s32[]{:T(128)}) while((s32[]{:T(128)}, bf16[5,512,4,64]{1,3,2,0:T(8,128)(2,1)S(1)}, f32[5,4,512]{2,1,0:T(4,128)}, bf16[5,512,3,4,64]{1,4,3,2,0:T(8,128)(2,1)}, ...), condition=%wide.region_4.5_spmd, body=%wide.region_1.4_spmd.sunk | while | flops 281147904 | bytes 15272541 | solution.py:161
  178.9 5.6 fusion.61
  185.4 176.6 %reduce-scatter.15.cloned.1.call-done = f32[640,1024]{1,0:T(8,128)} async-done(((f32[2560,1024]{1,0:T(8,128)}), f32[640,1024]{1,0:T(8,128)}) %reduce-scatter.15.cloned.1.call-update) | async-done | bytes 2621456 | tf_op jit(solution)/shard_map/reduce_scatter | solution.py:166
  362.0 2.9 fusion.59
  365.4 1.5 fusion.45
  367.6 8.9 all-gather.1
  376.6 16.5 %all-gather.13.cloned.1.call-done = bf16[1024,1024]{1,0:T(8,128)(2,1)} async-done(((bf16[1024,128]{1,0:T(8,128)(2,1)}), bf16[1024,1024]{1,0:T(8,128)(2,1)}) %all-gather.13.cloned.1.call-update) | async-done | bytes 2097168 | tf_op jit(solution)/shard_map/all_gather | solution.py:122
  393.1 100.1 %all-gather.11.cloned.1.call-done = bf16[2560,1024]{1,0:T(8,128)(2,1)} async-done(((bf16[640,1024]{1,0:T(8,128)(2,1)}), bf16[2560,1024]{1,0:T(8,128)(2,1)}) %all-gather.11.cloned.1.call-update) | async-done | bytes 5242896 | tf_op jit(solution)/shard_map/all_gather | solution.py:176
  493.1 32.2 %multiply_convert_fusion.1 = (bf16[2560,1024]{1,0:T(8,128)(2,1)}, f32[2560,1024]{1,0:T(8,128)}, f32[2560,1024]{1,0:T(8,128)}) fusion(f32[1024]{0:T(1024)S(1)} %bitcast.195, bf16[2560,1024]{1,0:T(8,128)(2,1)} %all-gather.11.cloned.1.call-done, bf16[1024,1024]{1,0:T(8,128)(2,1)} %all-gather.13.cloned.1.call-done), kind=kOutput, calls=%fused_computation.56 | convolution fusion | flops 5541724160 | bytes 33558528 | tf_op jit(solution)/shard_map/dot_general | solution.py:31
  525.3 10.2 convolution_convert_fusion.1
  535.8 92.0 %reduce-scatter.17.cloned.1.call-done = bf16[640,1024]{1,0:T(8,128)(2,1)} async-done(((bf16[2560,1024]{1,0:T(8,128)(2,1)}), bf16[640,1024]{1,0:T(8,128)(2,1)}) %reduce-scatter.17.cloned.1.call-update) | async-done | bytes 1310736 | tf_op jit(solution)/shard_map/reduce_scatter | solution.py:181
  627.8 2.3 fusion.57
  632.1 2.1 fusion.56
  635.7 1.9 convert_reduce_fusion.3
  637.8 98.7 %all-gather.17.cloned.1.call-done = bf16[2560,1024]{1,0:T(8,128)(2,1)} async-done(((bf16[640,1024]{1,0:T(8,128)(2,1)}), bf16[2560,1024]{1,0:T(8,128)(2,1)}) %all-gather.17.cloned.1.call-update) | async-done | bytes 5242896 | tf_op jit(solution)/shard_map/all_gather | solution.py:196
  736.4 16.5 %convert_reduce_fusion = (f32[1024]{0:T(1024)S(1)}, bf16[2560,1024]{1,0:T(8,128)(2,1)S(1)}) fusion(f32[2560,1024]{1,0:T(8,128)} %get-tuple-element.266, f32[2560,1024]{1,0:T(8,128)} %get-tuple-element.278, f32[1024]{0:T(1024)S(1)} %bitcast.196, bf16[2560,1024]{1,0:T(8,128)(2,1)} %all-gather.17.cloned.1.call-done, ...), kind=kOutput, calls=%fused_computation.54 | convolution fusion | flops 5413272576 | bytes 33562624 | tf_op jit(solution)/shard_map/dot_general | solution.py:31
  753.0 2.4 copy-done.27
  755.4 7.3 convolution_convert_fusion
  762.7 92.2 %reduce-scatter.19.cloned.1.call-done = bf16[640,1024]{1,0:T(8,128)(2,1)} async-done(((bf16[2560,1024]{1,0:T(8,128)(2,1)}), bf16[640,1024]{1,0:T(8,128)(2,1)}) %reduce-scatter.19.cloned.1.call-update) | async-done | bytes 1310736 | tf_op jit(solution)/shard_map/reduce_scatter | solution.py:202
  855.0 3.5 multiply_reduce_fusion.1
  863.4 97.8 %all-gather.19.cloned.1.call-done = bf16[2560,1024]{1,0:T(8,128)(2,1)} async-done(((bf16[640,1024]{1,0:T(8,128)(2,1)}), bf16[2560,1024]{1,0:T(8,128)(2,1)}) %all-gather.19.cloned.1.call-update) | async-done | bytes 5242896 | tf_op jit(solution)/shard_map/all_gather | solution.py:211
  961.2 5.1 convolution_convert_fusion.2
  966.3 4.3 reshape.259
  970.6 3.0 copy.99
  973.7 60.0 %while.23 = (s32[]{:T(128)}, bf16[5,512,3,4,64]{1,4,3,2,0:T(8,128)(2,1)}, bf16[5,512,3,4,64]{1,4,3,2,0:T(8,128)(2,1)}, s32[5]{0:T(128)S(1)}, f32[5,4,512]{2,1,0:...) while((s32[]{:T(128)}, bf16[5,512,3,4,64]{1,4,3,2,0:T(8,128)(2,1)}, ...), condition=%wide.region_18.19_spmd, body=%wide.region_16.18_spmd.sunk | while | flops 689830400 | bytes 37285476 | solution.py:214
  977.5 2.4 multiply_reduce_fusion.7
  982.6 2.1 fusion.112
  989.5 2.4 multiply_reduce_fusion.7
  994.6 2.1 fusion.112
  1001.6 2.4 multiply_reduce_fusion.7
  1006.6 2.1 fusion.112
  1013.5 2.4 multiply_reduce_fusion.7
  1018.6 2.1 fusion.112
  1025.5 2.4 multiply_reduce_fusion.7
  1030.6 2.1 fusion.112
  1033.6 2.7 convert_reduce_fusion.1
  1036.4 7.7 copy.100
  1044.9 9.7 reshape.240
  1054.8 9.7 convolution_bitcast_fusion
  1064.6 8.3 bitcast_convert_fusion
  1072.9 10.5 fusion.64
  1083.5 10.5 fusion.63
  1094.1 5.9 fusion.62
  1102.8 33.2 %reduce-scatter.23.cloned.1.call-done = f32[3,128,256]{1,2,0:T(8,128)} async-done(((f32[3,1024,256]{1,2,0:T(8,128)}), f32[3,128,256]{1,2,0:T(8,128)}) %reduce-scatter.23.cloned.1.call-update) | async-done | bytes 393232 | tf_op jit(solution)/shard_map/reduce_scatter | solution.py:251
  1135.9 1.9 copy.102
  1137.9 94.2 %reduce-scatter.21.cloned.1.call-done = bf16[640,1024]{1,0:T(8,128)(2,1)} async-done(((bf16[2560,1024]{1,0:T(8,128)(2,1)}), bf16[640,1024]{1,0:T(8,128)(2,1)}) %reduce-scatter.21.cloned.1.call-update) | async-done | bytes 1310736 | tf_op jit(solution)/shard_map/reduce_scatter | solution.py:233
  1232.1 3.4 fusion.54
  1235.5 41.5 %all-reduce.8 = (f32[1024]{0:T(1024)S(1)}, f32[1024]{0:T(1024)S(1)}, f32[1024]{0:T(1024)S(1)}, f32[1024]{0:T(1024)S(1)}, f32[1024]{0:T(1024)S(1)}, /*index=5*/f3...) all-reduce(f32[1024]{0:T(1024)S(1)} %get-tuple-element.220, ...), channel_id=6, replica_groups=mesh['dp'=8,'mp'=4] {'dp','mp'}, use_global_device_ids=true, to_apply=%region_21.22.clone | all-reduce | flops 8192 | bytes 65536
  1281.7 6.0 reduce-scatter.29.cloned.1.call-done
  1287.6 54.8 %reduce-scatter.27.cloned.1.call-done = f32[1024,128]{1,0:T(8,128)} async-done(((f32[1024,1024]{1,0:T(8,128)}), f32[1024,128]{1,0:T(8,128)}) %reduce-scatter.27.cloned.1.call-update) | async-done | bytes 524304 | tf_op jit(solution)/shard_map/reduce_scatter | solution.py:254
  1342.5 39.6 %reduce-scatter.25.cloned.1.call-done = f32[256,128]{1,0:T(8,128)} async-done(((f32[256,1024]{1,0:T(8,128)}), f32[256,128]{1,0:T(8,128)}) %reduce-scatter.25.cloned.1.call-update) | async-done | bytes 131088 | tf_op jit(solution)/shard_map/reduce_scatter | solution.py:252
  (220 shorter events, 93.5 us)
Async XLA Ops:
  7.2 50.4 %copy-start.4 = (bf16[640,1024]{1,0:T(8,128)(2,1)S(1)}, bf16[640,1024]{1,0:T(8,128)(2,1)}, u32[]{:S(2)}) copy-start(bf16[640,1024]{1,0:T(8,128)(2,1)} %param.22) | copy-start | bytes 3932164
  7.2 104.5 %all-gather.9.cloned.1.call-start = ((), (), s32[]{:S(2)}) async-start(), calls=%async_computation.10 | async-start | bytes 1769472 | tf_op jit(solution)/shard_map/all_gather | solution.py:119
  8.1 353.9 %copy-start.9 = (f32[640]{0:T(1024)}, f32[640]{0:T(1024)S(1)}, u32[]{:S(2)}) copy-start(f32[640]{0:T(1024)S(1)} %select_reduce_fusion) | copy-start | bytes 7684
  10.9 35.0 %collective-permute-start = (bf16[640,1024]{1,0:T(8,128)(2,1)}, bf16[640,1024]{1,0:T(8,128)(2,1)S(1)}, u32[]{:S(2)}, u32[]{:S(2)}) collective-permute-start(bf16[640,1024]{1,0:T(8,128)(2,1)} %fusion.44), channel_id=1, source_target_pairs={{0,1},{1,2},{2,3},{3,0},{4,5},{5,6},{6,7},{7,4},{8,9},{9,10},{10,1... | collective-permute-start | bytes 3932168 | tf_op jit(solution)/shard_map/ppermute | solution.py:141
  14.0 348.0 %reduce-scatter.15.cloned.1.call-start = ((), (), s32[]{:S(2)}) async-start(), calls=%async_computation.11 | async-start | bytes 13107200 | tf_op jit(solution)/shard_map/reduce_scatter | solution.py:166
  14.1 59.1 %collective-permute-start.2 = (bf16[640,1024]{1,0:T(8,128)(2,1)}, bf16[640,1024]{1,0:T(8,128)(2,1)}, u32[]{:S(2)}, u32[]{:S(2)}) collective-permute-start(bf16[640,1024]{1,0:T(8,128)(2,1)} %fusion.44), channel_id=1, source_target_pairs={{1,0},{2,1},{3,2},{0,3},{5,4},{6,5},{7,6},{4,7},{9,8},{10,9},{11,1... | collective-permute-start | bytes 3932168 | tf_op jit(solution)/shard_map/ppermute | solution.py:143
  45.9 55.4 %collective-permute-start.1 = (bf16[640,1024]{1,0:T(8,128)(2,1)S(1)}, bf16[640,1024]{1,0:T(8,128)(2,1)}, u32[]{:S(2)}, u32[]{:S(2)}) collective-permute-start(bf16[640,1024]{1,0:T(8,128)(2,1)S(1)} %collective-permute-done), channel_id=1, source_target_pairs={{0,1},{1,2},{2,3},{3,0},{4,5},{5,6},{6,7},{7,4},{8,9},{9,10},{10,1... | collective-permute-start | bytes 3932168 | tf_op jit(solution)/shard_map/ppermute | solution.py:141
  133.1 12.1 copy-start.8
  176.4 8.0 copy-start.25
  177.8 1.1 copy-start.5
  184.4 177.6 %copy-start.12 = (f32[1024]{0:T(1024)S(1)}, f32[1024]{0:T(1024)}, u32[]{:S(2)}) copy-start(f32[1024]{0:T(1024)} %param.26) | copy-start | bytes 12292
  184.4 177.6 %copy-start.13 = (f32[1024]{0:T(1024)S(1)}, f32[1024]{0:T(1024)}, u32[]{:S(2)}) copy-start(f32[1024]{0:T(1024)} %param.25) | copy-start | bytes 12292
  184.4 177.6 %copy-start.21 = (f32[1024]{0:T(1024)S(1)}, f32[1024]{0:T(1024)}, u32[]{:S(2)}) copy-start(f32[1024]{0:T(1024)} %param.30) | copy-start | bytes 12292
  184.4 208.6 %all-gather.13.cloned.1.call-start = ((), (), s32[]{:S(2)}) async-start(), calls=%async_computation.13 | async-start | bytes 2359296 | tf_op jit(solution)/shard_map/all_gather | solution.py:122
  185.2 180.2 %copy-start.11 = (f32[1024]{0:T(1024)S(1)}, f32[1024]{0:T(1024)}, u32[]{:S(2)}) copy-start(f32[1024]{0:T(1024)} %param.31) | copy-start | bytes 12292
  185.2 180.2 %copy-start.14 = (f32[1024]{0:T(1024)S(1)}, f32[1024]{0:T(1024)}, u32[]{:S(2)}) copy-start(f32[1024]{0:T(1024)} %param.32) | copy-start | bytes 12292
  185.2 307.9 %all-gather.11.cloned.1.call-start = ((), (), s32[]{:S(2)}) async-start(), calls=%async_computation.12 | async-start | bytes 6553600 | tf_op jit(solution)/shard_map/all_gather | solution.py:176
  364.9 2.6 copy-start.22
  366.9 158.4 %all-gather.15.cloned.1.call-start = ((), (), s32[]{:S(2)}) async-start(), calls=%async_computation.14 | async-start | bytes 2359296 | tf_op jit(solution)/shard_map/all_gather | solution.py:123
  367.5 260.3 %reduce-scatter.17.cloned.1.call-start = ((), (), s32[]{:S(2)}) async-start(), calls=%async_computation.15 | async-start | bytes 6553600 | tf_op jit(solution)/shard_map/reduce_scatter | solution.py:181
  535.5 92.3 %copy-start.19 = (f32[1024]{0:T(1024)S(1)}, f32[1024]{0:T(1024)}, u32[]{:S(2)}) copy-start(f32[1024]{0:T(1024)} %param.36) | copy-start | bytes 12292
  535.6 95.0 %copy-start.15 = (f32[1024]{0:T(1024)S(1)}, f32[1024]{0:T(1024)}, u32[]{:S(2)}) copy-start(f32[1024]{0:T(1024)} %param.37) | copy-start | bytes 12292
  535.6 200.8 %all-gather.17.cloned.1.call-start = ((), (), s32[]{:S(2)}) async-start(), calls=%async_computation.16 | async-start | bytes 6553600 | tf_op jit(solution)/shard_map/all_gather | solution.py:196
  627.8 2.8 copy-start.6
  630.2 1.9 copy-start.20
  634.3 1.5 copy-start
  637.7 217.2 %reduce-scatter.19.cloned.1.call-start = ((), (), s32[]{:S(2)}) async-start(), calls=%async_computation.17 | async-start | bytes 6553600 | tf_op jit(solution)/shard_map/reduce_scatter | solution.py:202
  736.4 19.0 %copy-start.23 = (bf16[1024,1024]{1,0:T(8,128)(2,1)S(1)}, bf16[1024,1024]{1,0:T(8,128)(2,1)}, u32[]{:S(2)}) copy-start(bf16[1024,1024]{1,0:T(8,128)(2,1)} %all-gather.13.cloned.1.call-done) | copy-start | bytes 6291460
  753.0 2.4 copy-start.27
  762.7 198.5 %all-gather.19.cloned.1.call-start = ((), (), s32[]{:S(2)}) async-start(), calls=%async_computation.18 | async-start | bytes 6553600 | tf_op jit(solution)/shard_map/all_gather | solution.py:211
  855.0 3.5 copy-start.1
  855.0 3.5 copy-start.7
  859.6 1.5 copy-start.2
  862.5 237.6 %reduce-scatter.33.cloned.1.call-start = ((), (), s32[]{:S(2)}) async-start(), calls=%async_computation.25 | async-start | bytes 73728
  863.3 238.1 %reduce-scatter.31.cloned.1.call-start = ((), (), s32[]{:S(2)}) async-start(), calls=%async_computation.24 | async-start | bytes 73728
  966.3 7.3 copy-start.26
  1054.6 10.0 copy-start.24
  1054.6 81.3 %reduce-scatter.23.cloned.1.call-start = ((), (), s32[]{:S(2)}) async-start(), calls=%async_computation.20 | async-start | bytes 3538944 | tf_op jit(solution)/shard_map/reduce_scatter | solution.py:251
  1064.5 167.5 %reduce-scatter.21.cloned.1.call-start = ((), (), s32[]{:S(2)}) async-start(), calls=%async_computation.19 | async-start | bytes 6553600 | tf_op jit(solution)/shard_map/reduce_scatter | solution.py:233
  1072.9 214.8 %reduce-scatter.29.cloned.1.call-start = ((), (), s32[]{:S(2)}) async-start(), calls=%async_computation.23 | async-start | bytes 4718592 | tf_op jit(solution)/shard_map/reduce_scatter | solution.py:255
  1083.4 259.0 %reduce-scatter.27.cloned.1.call-start = ((), (), s32[]{:S(2)}) async-start(), calls=%async_computation.22 | async-start | bytes 4718592 | tf_op jit(solution)/shard_map/reduce_scatter | solution.py:254
  1094.0 138.1 %copy-start.3 = (f32[640,1024]{1,0:T(8,128)S(1)}, f32[640,1024]{1,0:T(8,128)}, u32[]{:S(2)}) copy-start(f32[640,1024]{1,0:T(8,128)} %copy-done.2) | copy-start | bytes 7864324
  1094.0 138.1 %copy-start.10 = (f32[640]{0:T(1024)S(1)}, f32[640]{0:T(1024)}, u32[]{:S(2)}) copy-start(f32[640]{0:T(1024)} %copy-done.9) | copy-start | bytes 7684
  1094.0 288.1 %reduce-scatter.25.cloned.1.call-start = ((), (), s32[]{:S(2)}) async-start(), calls=%async_computation.21 | async-start | bytes 1179648 | tf_op jit(solution)/shard_map/reduce_scatter | solution.py:252
  1100.0 135.5 %copy-start.16 = (f32[1024]{0:T(1024)S(1)}, f32[1024]{0:T(1024)}, u32[]{:S(2)}) copy-start(f32[1024]{0:T(1024)} %get-tuple-element.216) | copy-start | bytes 12292
  1100.0 135.5 %copy-start.17 = (f32[1024]{0:T(1024)S(1)}, f32[1024]{0:T(1024)}, u32[]{:S(2)}) copy-start(f32[1024]{0:T(1024)} %get-tuple-element.221) | copy-start | bytes 12292
  1100.0 135.5 %copy-start.18 = (f32[1024]{0:T(1024)S(1)}, f32[1024]{0:T(1024)}, u32[]{:S(2)}) copy-start(f32[1024]{0:T(1024)} %get-tuple-element.254) | copy-start | bytes 12292
Sparse Core Ops, SparseCore 0:
  14.1 25.7 all-gather.8
  184.6 177.3 reduce-scatter.14
  363.9 29.1 all-gather.12
  395.1 98.0 all-gather.10
  494.9 26.4 all-gather.14
  535.7 92.0 reduce-scatter.16
  637.8 98.5 all-gather.16
  762.8 92.0 reduce-scatter.18
  862.6 98.5 all-gather.18
  964.0 31.8 reduce-scatter.32
  1054.7 31.8 reduce-scatter.30
  1089.9 46.0 reduce-scatter.22
  1138.2 93.7 reduce-scatter.20
  1235.8 51.7 reduce-scatter.28
  1291.4 51.0 reduce-scatter.26
  1346.1 35.9 reduce-scatter.24
